TPU v7x, 128 devices: a whole 4x4x4 slice. The times are simulated.
128 devices in a mesh: gz: 4 (over z), xy: 32 (over x, y, core).
Axes of the slice: x: 4, y: 4, z: 4, core: 2. Of those that a mesh axis runs over, the one named last changes fastest.
Arguments:
- source_inner: float32 [8, 2, 16, 16384], P('gz', None, None, 'xy'), may hold values from -6 to 6
- source_front: float32 [8, 2, 16, 4096], P('gz', None, None, 'xy'), may hold values from -6 to 6
- inner_inverse: bfloat16 [8, 32, 2, 512, 512], P('gz', 'xy'), may hold values from -0.1875 to 0.1875
- coupling: bfloat16 [8, 32, 2, 512, 256], P('gz', 'xy'), may hold values from -0.1875 to 0.1875
- schur_inverse: bfloat16 [8, 2, 4096, 4096], P('gz', None, None, 'xy'), may hold values from -0.046875 to 0.046875
- front_rows: int32 [8, 8192], P('gz', 'xy'), may hold values from 0 to 4095, as said below
- link: float32 [8, 4096], P('gz', 'xy'), may hold values from 0.5 to 1.5
- front_size: int32 [8], P('gz'), may hold values from 2048 to 4096, as said below
Outputs:
- inner_field: float32 [8, 2, 16, 16384], P('gz', None, None, 'xy')
- front_field: float32 [8, 2, 16, 4096], P('gz', None, None, 'xy')
Inputs may be any that keep to these rules, and one draw needn't show every extreme that they name: `front_rows`: within one local front of one panel the 256 entries are distinct. `front_size`: some panel has exactly 4096 live unknowns and some exactly half of 4096.
All inputs are finite; a program needn't handle non-finite values.
Results may differ from a plain program's by a relative error of at most 0.0075.
Values may be sent and summed in bfloat16 or wider, within the bound.
A program may use at most 64 MiB of HBM per device.

v0:
```python
import jax
import jax.numpy as jnp
from jax import lax
from jax.sharding import PartitionSpec as P


def passed_along(shard, axis, by):
    peers = lax.axis_size(axis)
    pairs = [(i, i + by) for i in range(peers) if 0 <= i + by < peers]
    return lax.ppermute(shard, axis, pairs)


def complex_product(field, matrix):
    row_count = field.shape[1]
    flattened = field.astype(jnp.bfloat16).reshape(2 * row_count, field.shape[2])
    first_part = jnp.dot(flattened, matrix[0], preferred_element_type=jnp.float32)
    second = jnp.dot(flattened, matrix[1], preferred_element_type=jnp.float32)
    return jnp.stack(
        [first_part[:row_count] - second[row_count:], second[:row_count] + first_part[row_count:]]
    )


def complex_product_t(field, matrix):
    row_count = field.shape[1]
    flattened = field.reshape(2 * row_count, field.shape[2])
    contract = (((1,), (1,)), ((), ()))
    first_part = lax.dot_general(flattened, matrix[0], contract, preferred_element_type=jnp.float32)
    second = lax.dot_general(flattened, matrix[1], contract, preferred_element_type=jnp.float32)
    return jnp.stack(
        [first_part[:row_count] - second[row_count:], second[:row_count] + first_part[row_count:]]
    )


def schur_apply(rhs_front, matrix):
    outgoing = rhs_front.astype(jnp.bfloat16)
    return complex_product(lax.all_gather(outgoing, "xy", axis=2, tiled=True), matrix)


def on_device(
    source_inner, source_front, inner_inverse, coupling, schur_inverse, front_rows, link, front_size
):
    chain_length = lax.axis_size("gz")
    panel_count = source_inner.shape[0]
    side_count = source_inner.shape[2]
    share_rows = source_front.shape[3]
    own_start = lax.axis_index("xy") * share_rows
    own_rows = own_start + jnp.arange(share_rows, dtype=jnp.int32)
    masks = [
        (own_rows < front_size[panel_index]).astype(jnp.float32)
        for panel_index in range(panel_count)
    ]
    solved_all = []
    bases = []
    for panel_index in range(panel_count):
        solved = complex_product(source_inner[panel_index], inner_inverse[panel_index, 0])
        pushed = complex_product(solved, coupling[panel_index, 0])
        spread = jnp.zeros((2, side_count, share_rows * lax.axis_size("xy")), jnp.float32)
        spread = spread.at[:, :, front_rows[panel_index]].add(pushed)
        contrib = lax.psum_scatter(spread, "xy", scatter_dimension=2, tiled=True)
        solved_all.append(solved)
        bases.append(source_front[panel_index] - contrib)
    incoming = jnp.zeros((2, side_count, share_rows), jnp.float32)
    for turn_index in range(chain_length):
        if turn_index > 0:
            incoming = passed_along(outgoing, "gz", 1)
        forward_incoming = incoming
        forward_results = []
        for forward_panel_index in range(panel_count):
            base_rhs = bases[forward_panel_index]
            rhs_front = masks[forward_panel_index] * (
                base_rhs + link[forward_panel_index] * forward_incoming
            )
            forward_incoming = masks[forward_panel_index] * schur_apply(
                rhs_front, schur_inverse[forward_panel_index]
            )
            forward_results.append(forward_incoming)
        fronts = forward_results
        outgoing = fronts[-1]
    incoming = jnp.zeros((2, side_count, share_rows), jnp.float32)
    for turn_index in range(chain_length):
        if turn_index > 0:
            incoming = passed_along(outgoing, "gz", -1)
        backward_incoming = incoming
        results = [None] * panel_count
        for backward_panel_index in reversed(range(panel_count)):
            change = masks[backward_panel_index] * schur_apply(
                masks[backward_panel_index] * backward_incoming, schur_inverse[backward_panel_index]
            )
            results[backward_panel_index] = change
            backward_incoming = link[backward_panel_index] * (fronts[backward_panel_index] + change)
        changes = results
        outgoing = backward_incoming
    totals = [fronts[panel_index] + changes[panel_index] for panel_index in range(panel_count)]
    stacked = jnp.stack(totals)
    everywhere = lax.all_gather(stacked.astype(jnp.bfloat16), "xy", axis=3, tiled=True)
    inner_out = []
    for panel_index in range(panel_count):
        picked = jnp.take(everywhere[panel_index], front_rows[panel_index], axis=2)
        lifted = complex_product_t(picked, coupling[panel_index, 0])
        inner_out.append(
            solved_all[panel_index] - complex_product(lifted, inner_inverse[panel_index, 0])
        )
    return (jnp.stack(inner_out), stacked)


def solution(mesh):
    placed = (
        P("gz", None, None, "xy"),
        P("gz", None, None, "xy"),
        P("gz", "xy", None, None, None),
        P("gz", "xy", None, None, None),
        P("gz", None, None, "xy"),
        P("gz", "xy"),
        P("gz", "xy"),
        P("gz"),
    )
    return jax.shard_map(
        on_device,
        mesh=mesh,
        in_specs=placed,
        out_specs=(P("gz", None, None, "xy"), P("gz", None, None, "xy")),
        check_vma=False,
    )
```

profile of v0, /device:TPU:1, one launch (start us, length us, event | category | flops | bytes accessed | tf_op | source)
XLA Modules:
  0.0 632.3 jit_solution(10690128480928282529)
XLA Ops:
  14.4 2.9 broadcast.94.clone
  17.3 24.7 %scatter_fusion = f32[2,16,4096]{1,0,2:T(2,128)} fusion(f32[2,16,4096]{1,0,2:T(2,128)} %broadcast.94.clone, s32[256]{0:T(256)S(1)} %bitcast.374, f32[256,2,16]{2,1,0:T(2,128)S(1)} %copy.20), kind=kCustom, calls=%fused_computation.2 | custom fusion | flops 8192 | bytes 99328 | tf_op jit(solution)/shard_map/scatter-add | solution.py:58
  42.0 5.8 copy.21
  49.5 2.9 broadcast.94.clone.1
  52.4 24.9 %scatter_fusion.1 = f32[2,16,4096]{1,0,2:T(2,128)} fusion(f32[2,16,4096]{1,0,2:T(2,128)} %broadcast.94.clone.1, s32[256]{0:T(256)S(1)} %bitcast.373, f32[256,2,16]{2,1,0:T(2,128)S(1)} %copy.22), kind=kCustom, calls=%fused_computation.3 | custom fusion | flops 8192 | bytes 99328 | tf_op jit(solution)/shard_map/scatter-add | solution.py:58
  77.2 5.9 copy.23
  88.1 38.5 %reduce-scatter.3.cloned.1.call-done = f32[2,16,128]{2,1,0:T(8,128)} async-done(((f32[2,16,4096]{2,1,0:T(8,128)}), f32[2,16,128]{2,1,0:T(8,128)}) %reduce-scatter.3.cloned.1.call-update) | async-done | bytes 16400 | tf_op jit(solution)/shard_map/reduce_scatter | solution.py:59
  127.4 26.2 %all_gather.49 = bf16[2,16,4096]{2,1,0:T(8,128)(2,1)S(1)} all-gather(bf16[2,16,128]{2,1,0:T(8,128)(2,1)S(1)} %get-tuple-element.7), channel_id=1, replica_groups=mesh['gz'=4,'xy'=32] {'xy'}, dimensions={2}, use_global_device_ids=true | all-gather | bytes 270336 | tf_op jit(solution)/shard_map/all_gather | solution.py:36
  156.6 50.2 %reduce-scatter.5.cloned.1.call-done = f32[2,16,128]{2,1,0:T(8,128)} async-done(((f32[2,16,4096]{2,1,0:T(8,128)}), f32[2,16,128]{2,1,0:T(8,128)}) %reduce-scatter.5.cloned.1.call-update) | async-done | bytes 16400 | tf_op jit(solution)/shard_map/reduce_scatter | solution.py:59
  207.7 26.3 %all_gather.50 = bf16[2,16,4096]{2,1,0:T(8,128)(2,1)S(1)} all-gather(bf16[2,16,128]{2,1,0:T(8,128)(2,1)S(1)} %get-tuple-element.5), channel_id=1, replica_groups=mesh['gz'=4,'xy'=32] {'xy'}, dimensions={2}, use_global_device_ids=true | all-gather | bytes 270336 | tf_op jit(solution)/shard_map/all_gather | solution.py:36
  237.1 3.2 collective-permute-start
  241.1 23.1 %all_gather.51 = bf16[2,16,4096]{2,1,0:T(8,128)(2,1)S(1)} all-gather(bf16[2,16,128]{2,1,0:T(8,128)(2,1)S(1)} %multiply_convert_fusion.6), channel_id=1, replica_groups=mesh['gz'=4,'xy'=32] {'xy'}, dimensions={2}, use_global_device_ids=true | all-gather | bytes 270336 | tf_op jit(solution)/shard_map/all_gather | solution.py:36
  266.1 23.8 %all_gather.52 = bf16[2,16,4096]{2,1,0:T(8,128)(2,1)S(1)} all-gather(bf16[2,16,128]{2,1,0:T(8,128)(2,1)S(1)} %fusion.171), channel_id=1, replica_groups=mesh['gz'=4,'xy'=32] {'xy'}, dimensions={2}, use_global_device_ids=true | all-gather | bytes 270336 | tf_op jit(solution)/shard_map/all_gather | solution.py:36
  290.6 4.0 collective-permute-start.1
  295.4 23.1 %all_gather.53 = bf16[2,16,4096]{2,1,0:T(8,128)(2,1)S(1)} all-gather(bf16[2,16,128]{2,1,0:T(8,128)(2,1)S(1)} %multiply_convert_fusion.5), channel_id=1, replica_groups=mesh['gz'=4,'xy'=32] {'xy'}, dimensions={2}, use_global_device_ids=true | all-gather | bytes 270336 | tf_op jit(solution)/shard_map/all_gather | solution.py:36
  319.1 23.8 %all_gather.54 = bf16[2,16,4096]{2,1,0:T(8,128)(2,1)S(1)} all-gather(bf16[2,16,128]{2,1,0:T(8,128)(2,1)S(1)} %fusion.175), channel_id=1, replica_groups=mesh['gz'=4,'xy'=32] {'xy'}, dimensions={2}, use_global_device_ids=true | all-gather | bytes 270336 | tf_op jit(solution)/shard_map/all_gather | solution.py:36
  343.6 4.0 collective-permute-start.2
  348.4 23.1 %all_gather.55 = bf16[2,16,4096]{2,1,0:T(8,128)(2,1)S(1)} all-gather(bf16[2,16,128]{2,1,0:T(8,128)(2,1)S(1)} %multiply_convert_fusion.4), channel_id=1, replica_groups=mesh['gz'=4,'xy'=32] {'xy'}, dimensions={2}, use_global_device_ids=true | all-gather | bytes 270336 | tf_op jit(solution)/shard_map/all_gather | solution.py:36
  372.2 23.8 %all_gather.56 = bf16[2,16,4096]{2,1,0:T(8,128)(2,1)S(1)} all-gather(bf16[2,16,128]{2,1,0:T(8,128)(2,1)S(1)} %multiply_convert_fusion.3), channel_id=1, replica_groups=mesh['gz'=4,'xy'=32] {'xy'}, dimensions={2}, use_global_device_ids=true | all-gather | bytes 270336 | tf_op jit(solution)/shard_map/all_gather | solution.py:36
  396.6 22.5 %all_gather.57 = bf16[2,16,4096]{2,1,0:T(8,128)(2,1)S(1)} all-gather(bf16[2,16,128]{2,1,0:T(8,128)(2,1)S(1)} %fusion.180), channel_id=1, replica_groups=mesh['gz'=4,'xy'=32] {'xy'}, dimensions={2}, use_global_device_ids=true | all-gather | bytes 270336 | tf_op jit(solution)/shard_map/all_gather | solution.py:36
  421.6 3.2 collective-permute-done.3
  424.8 24.7 %all_gather.58 = bf16[2,16,4096]{2,1,0:T(8,128)(2,1)S(1)} all-gather(bf16[2,16,128]{2,1,0:T(8,128)(2,1)S(1)} %multiply_convert_fusion.2), channel_id=1, replica_groups=mesh['gz'=4,'xy'=32] {'xy'}, dimensions={2}, use_global_device_ids=true | all-gather | bytes 270336 | tf_op jit(solution)/shard_map/all_gather | solution.py:36
  450.1 22.3 %all_gather.59 = bf16[2,16,4096]{2,1,0:T(8,128)(2,1)S(1)} all-gather(bf16[2,16,128]{2,1,0:T(8,128)(2,1)S(1)} %fusion.186), channel_id=1, replica_groups=mesh['gz'=4,'xy'=32] {'xy'}, dimensions={2}, use_global_device_ids=true | all-gather | bytes 270336 | tf_op jit(solution)/shard_map/all_gather | solution.py:36
  474.3 3.4 collective-permute-done.4
  477.8 24.7 %all_gather.60 = bf16[2,16,4096]{2,1,0:T(8,128)(2,1)S(1)} all-gather(bf16[2,16,128]{2,1,0:T(8,128)(2,1)S(1)} %multiply_convert_fusion.1), channel_id=1, replica_groups=mesh['gz'=4,'xy'=32] {'xy'}, dimensions={2}, use_global_device_ids=true | all-gather | bytes 270336 | tf_op jit(solution)/shard_map/all_gather | solution.py:36
  503.1 22.3 %all_gather.61 = bf16[2,16,4096]{2,1,0:T(8,128)(2,1)S(1)} all-gather(bf16[2,16,128]{2,1,0:T(8,128)(2,1)S(1)} %fusion.192), channel_id=1, replica_groups=mesh['gz'=4,'xy'=32] {'xy'}, dimensions={2}, use_global_device_ids=true | all-gather | bytes 270336 | tf_op jit(solution)/shard_map/all_gather | solution.py:36
  530.8 24.7 %all_gather.62 = bf16[2,16,4096]{2,1,0:T(8,128)(2,1)S(1)} all-gather(bf16[2,16,128]{2,1,0:T(8,128)(2,1)S(1)} %multiply_convert_fusion), channel_id=1, replica_groups=mesh['gz'=4,'xy'=32] {'xy'}, dimensions={2}, use_global_device_ids=true | all-gather | bytes 270336 | tf_op jit(solution)/shard_map/all_gather | solution.py:36
  556.1 22.3 %all_gather.63 = bf16[2,16,4096]{2,1,0:T(8,128)(2,1)S(1)} all-gather(bf16[2,16,128]{2,1,0:T(8,128)(2,1)S(1)} %fusion.198), channel_id=1, replica_groups=mesh['gz'=4,'xy'=32] {'xy'}, dimensions={2}, use_global_device_ids=true | all-gather | bytes 270336 | tf_op jit(solution)/shard_map/all_gather | solution.py:36
  579.7 24.2 %all_gather.64 = bf16[2,2,16,4096]{3,2,1,0:T(8,128)(2,1)S(1)} all-gather(bf16[2,2,16,128]{3,2,1,0:T(8,128)(2,1)S(1)} %get-tuple-element.3), channel_id=1, replica_groups=mesh['gz'=4,'xy'=32] {'xy'}, dimensions={3}, use_global_device_ids=true | all-gather | bytes 540672 | tf_op jit(solution)/shard_map/all_gather | solution.py:95
  604.6 5.0 copy.24
  609.6 3.2 gather_fusion
  614.9 3.8 copy.26
  (152 shorter events, 50.8 us)
Async XLA Ops:
  7.2 119.5 %reduce-scatter.3.cloned.1.call-start = ((), (), s32[]{:S(2)}) async-start(), calls=%async_computation.2 | async-start | bytes 540672 | tf_op jit(solution)/shard_map/reduce_scatter | solution.py:59
  14.4 33.5 %copy-start.1 = (bf16[2,1,2,512,512]{4,3,2,1,0:T(8,128)(2,1)S(1)}, bf16[2,1,2,512,512]{4,3,2,1,0:T(8,128)(2,1)}, u32[]{:S(2)}) copy-start(bf16[2,1,2,512,512]{4,3,2,1,0:T(8,128)(2,1)} %param.12) | copy-start | bytes 6291460
  17.3 31.7 %copy-start.2 = (bf16[2,1,2,512,256]{4,3,2,1,0:T(8,128)(2,1)S(1)}, bf16[2,1,2,512,256]{4,3,2,1,0:T(8,128)(2,1)}, u32[]{:S(2)}) copy-start(bf16[2,1,2,512,256]{4,3,2,1,0:T(8,128)(2,1)} %param.13) | copy-start | bytes 3145732
  47.9 158.9 %reduce-scatter.5.cloned.1.call-start = ((), (), s32[]{:S(2)}) async-start(), calls=%async_computation.3 | async-start | bytes 540672 | tf_op jit(solution)/shard_map/reduce_scatter | solution.py:59
  49.5 33.7 %copy-start.6 = (f32[2,128]{1,0:T(2,128)S(1)}, f32[2,128]{1,0:T(2,128)}, u32[]{:S(2)}) copy-start(f32[2,128]{1,0:T(2,128)} %param.16) | copy-start | bytes 3076
  52.4 33.8 %copy-start.4 = (s32[2,256]{1,0:T(2,128)S(1)}, s32[2,256]{1,0:T(2,128)}, u32[]{:S(2)}) copy-start(s32[2,256]{1,0:T(2,128)} %param.15) | copy-start | bytes 6148
  52.4 33.8 %copy-start.5 = (s32[2]{0:T(128)S(1)}, s32[2]{0:T(128)}, u32[]{:S(2)}) copy-start(s32[2]{0:T(128)} %param.17) | copy-start | bytes 28
  52.4 74.3 %copy-start.3 = (f32[2,2,16,128]{3,2,1,0:T(8,128)S(1)}, f32[2,2,16,128]{3,2,1,0:T(8,128)}, u32[]{:S(2)}) copy-start(f32[2,2,16,128]{3,2,1,0:T(8,128)} %param.11) | copy-start | bytes 98308
  206.8 59.0 %copy-start = (bf16[2,2,4096,128]{3,2,1,0:T(8,128)(2,1)S(1)}, bf16[2,2,4096,128]{3,2,1,0:T(8,128)(2,1)}, u32[]{:S(2)}) copy-start(bf16[2,2,4096,128]{3,2,1,0:T(8,128)(2,1)} %param.14) | copy-start | bytes 12582916
  237.1 4.0 collective-permute-start
  290.6 4.8 collective-permute-start.1
  343.6 4.8 collective-permute-start.2
  419.7 5.1 collective-permute-start.3
  473.0 4.8 collective-permute-start.4
  526.0 4.8 collective-permute-start.5
Sparse Core Ops, SparseCore 0:
  48.0 78.5 reduce-scatter.2
  130.1 76.6 reduce-scatter.4
where the time goes:
time: 635 us; the launch traced here: 632 us
  blocking collectives  381 us (60%)
  waiting for transfers between devices  101 us (16%)
  other arithmetic  62 us (10%)
  local copies, waits for them, and re-layouts  34 us (5%)
  matrix products  24.5 us (4%)
  starting transfers between devices  15 us (2%)
  between operations  14.8 us (2%)
    all_gather x15, blocking collectives, schur_apply(): lax.all_gather(outgoing, 'xy', axis=2, tiled=True)  357 us
    reduce_scatter x2, waiting for transfers between devices, on_device(): contrib = lax.psum_scatter(spread, 'xy', scatter_dimension=2, tiled=True)  88.7 us
    scatter-add x2, other arithmetic, on_device(): spread = spread.at[:, :, front_rows[panel_index]].add(pushed)  49.6 us
    all_gather x1, blocking collectives, on_device(): lax.all_gather(stacked.astype(jnp.bfloat16), 'xy', axis=3, tiled=True)  24.2 us
    ppermute x6, starting transfers between devices, passed_along(): return lax.ppermute(shard, axis, pairs)  15 us
  transfers between devices with their start and end apart: 8, of which 8 were waited for; matrix products, arithmetic and copies ran while one was open for 7% of the time, Pallas kernels for 0%

commit v1 on v0

v1 whole, which is shorter than its diff:
```python
import functools

import jax
import jax.numpy as jnp
from jax import lax
from jax.experimental import pallas as pl
from jax.experimental.pallas import tpu as pltpu
from jax.sharding import PartitionSpec as P

MESH = pl.DeviceIdType.MESH
F32 = jnp.float32
BF16 = jnp.bfloat16
NT = (((1,), (1,)), ((), ()))
LANES = 128

FWD0, FWD1, BWD1, BWD0, TOT1, TOT0 = range(6)


def dot(a, b):
    return jnp.dot(a, b, preferred_element_type=F32)


def combined(first, second):
    half = first.shape[0] // 2
    return jnp.concatenate([first[:half] - second[half:], second[:half] + first[half:]], axis=0)


def kernel(
    side,
    depth,
    inner_hbm,
    front_hbm,
    inverse_hbm,
    coupling_hbm,
    schur_hbm,
    rows_hbm,
    link_hbm,
    size_ref,
    inner_out,
    front_out,
    inner_v,
    front_v,
    inverse_v,
    coupling_v,
    schur_v,
    rows_v,
    link_v,
    onehot,
    parts,
    landed,
    gathered,
    passed,
    passing,
    solved_v,
    inner_res,
    front_res,
    base_v,
    load_sem,
    store_sem,
    send_sem,
    gather_sem,
    contrib_sem,
    pass_send_sem,
    pass_recv_sem,
):
    chips = side * side
    peers = 2 * chips
    me = lax.axis_index("xy")
    turn = lax.axis_index("gz")
    core = lax.rem(me, 2)
    chip = me // 2
    chip_x = chip // side
    chip_y = lax.rem(chip, side)

    def chip_at(dx, dy):
        return lax.rem(chip_x + dx, side) * side + lax.rem(chip_y + dy, side)

    def distance(d):
        return min(d, side - d)

    offsets = sorted(
        ((dx, dy) for dx in range(side) for dy in range(side)),
        key=lambda d: (distance(d[0]) + distance(d[1]), d),
    )
    near_chips = [chip_at(*d) for d in offsets]
    far_first = [
        2 * c + lax.rem(core + q, 2) for c in reversed(near_chips[1:]) for q in range(2)
    ] + [2 * chip + 1 - core]

    loads = []

    def load(src, dst):
        copy = pltpu.make_async_copy(src, dst, load_sem.at[len(loads)])
        copy.start()
        loads.append(copy)
        return copy

    rows_load = load(rows_hbm, rows_v)
    inner_load = load(inner_hbm, inner_v)
    local_loads = []
    for p in range(2):
        local_loads.append((load(inverse_hbm.at[p], inverse_v.at[p]), load(coupling_hbm.at[p], coupling_v.at[p])))
    front_load = load(front_hbm, front_v)
    link_load = load(link_hbm, link_v)
    schur_loads = [
        [load(schur_hbm.at[p, i], schur_v.at[p, :, pl.ds(i * LANES, LANES)]) for i in range(2)]
        for p in range(2)
    ]

    barrier = pltpu.get_barrier_semaphore()
    for peer in far_first:
        pl.semaphore_signal(barrier, inc=1, device_id={"xy": peer}, device_id_type=MESH)

    @pl.when(turn > 0)
    def _():
        pl.semaphore_signal(barrier, inc=1, device_id={"gz": turn - 1}, device_id_type=MESH)

    @pl.when(turn < depth - 1)
    def _():
        pl.semaphore_signal(barrier, inc=1, device_id={"gz": turn + 1}, device_id_type=MESH)

    def local_part(p):
        iota = lax.broadcasted_iota(jnp.int32, (2 * LANES, 2 * LANES), 0)
        wanted = rows_v[p : p + 1, :]
        for c in range(chips):
            onehot[p, pl.ds(c * 2 * LANES, 2 * LANES), :] = (
                iota + c * 2 * LANES == wanted
            ).astype(F32).astype(BF16)
        for copy in local_loads[p]:
            copy.wait()
        field = inner_v[p].reshape(-1, inner_v.shape[-1]).astype(BF16)
        solved = combined(dot(field, inverse_v[p, 0]), dot(field, inverse_v[p, 1]))
        solved_v[p] = solved
        rounded = solved.astype(BF16)
        pushed = combined(dot(rounded, coupling_v[p, 0]), dot(rounded, coupling_v[p, 1])).astype(BF16)
        for c in range(chips):
            spread = lax.dot_general(
                pushed, onehot[p, pl.ds(c * 2 * LANES, 2 * LANES), :], NT, preferred_element_type=F32
            ).astype(BF16)
            parts[p, 2 * c] = spread[:, :LANES]
            parts[p, 2 * c + 1] = spread[:, LANES:]
        landed[p, me] = parts[p, me]

    def send_parts(p):
        for peer in far_first:
            pltpu.make_async_remote_copy(
                src_ref=parts.at[p, peer],
                dst_ref=landed.at[p, me],
                send_sem=send_sem.at[p],
                recv_sem=contrib_sem.at[p],
                device_id={"xy": peer},
                device_id_type=MESH,
            ).start()

    def wait_bytes(ref, sem):
        pltpu.make_async_copy(ref, ref, sem).wait()

    rows_load.wait()
    inner_load.wait()
    local_part(0)
    pl.semaphore_wait(barrier, peers - 1 + jnp.minimum(turn, 1) + jnp.minimum(depth - 1 - turn, 1))
    send_parts(0)
    local_part(1)
    send_parts(1)

    front_load.wait()
    link_load.wait()
    for p in range(2):
        wait_bytes(landed.at[p, pl.ds(0, peers - 1)], contrib_sem.at[p])
        total = landed[p, 0].astype(F32)
        for i in range(1, peers):
            total = total + landed[p, i].astype(F32)
        base_v[p] = front_v[p].reshape(total.shape) - total
        for copy in schur_loads[p]:
            copy.wait()

    own = me * LANES + lax.broadcasted_iota(jnp.int32, (1, LANES), 1)
    masks = [jnp.where(own < size_ref[p], 1.0, 0.0).astype(F32) for p in range(2)]
    links = [link_v[p : p + 1, :] for p in range(2)]

    def share(g, block):
        gathered[g, me] = block.astype(BF16)
        for peer in far_first:
            pltpu.make_async_remote_copy(
                src_ref=gathered.at[g, me],
                dst_ref=gathered.at[g, me],
                send_sem=send_sem.at[2 + g],
                recv_sem=gather_sem.at[g, chip],
                device_id={"xy": peer},
                device_id_type=MESH,
            ).start()

    def product(g, matrix, waits=True):
        total = None
        for i, c in enumerate(near_chips):
            if waits:
                if i == 0:
                    wait_bytes(gathered.at[g, 0], gather_sem.at[g, c])
                else:
                    wait_bytes(gathered.at[g, pl.ds(0, 2)], gather_sem.at[g, c])
            block = jnp.concatenate([gathered[g, 2 * c], gathered[g, 2 * c + 1]], axis=1)
            rows = pl.ds(pl.multiple_of(c * 2 * LANES, 2 * LANES), 2 * LANES)
            term = dot(block, matrix[rows, :])
            total = term if total is None else total + term
        return total

    def schur(g, p, waits=True):
        out = product(g, schur_v.at[p], waits)
        return combined(out[:, :LANES], out[:, LANES:])

    def hand_on(i, to):
        return pltpu.make_async_remote_copy(
            src_ref=passing.at[i],
            dst_ref=passed.at[i],
            send_sem=pass_send_sem.at[i],
            recv_sem=pass_recv_sem.at[i],
            device_id={"gz": to},
            device_id_type=MESH,
        )

    @pl.when(turn == 0)
    def _():
        passed[0] = jnp.zeros_like(passed[0])

    @pl.when(turn == depth - 1)
    def _():
        for i in range(peers):
            gathered[BWD1, i] = jnp.zeros_like(gathered[BWD1, i])
        front_res[1] = schur(BWD1, 1, waits=False)

    @pl.when(turn > 0)
    def _():
        hand_on(0, turn - 1).wait_recv()

    share(FWD0, masks[0] * (base_v[0] + links[0] * passed[0]))
    front0 = masks[0] * schur(FWD0, 0)
    share(FWD1, masks[1] * (base_v[1] + links[1] * front0))
    front1 = masks[1] * schur(FWD1, 1)

    @pl.when(turn < depth - 1)
    def _():
        passing[0] = front1
        hand_on(0, turn + 1).start()

    @pl.when(turn < depth - 1)
    def _():
        hand_on(1, turn + 1).wait_recv()
        share(BWD1, masks[1] * passed[1])
        front_res[1] = schur(BWD1, 1)

    total1 = front1 + masks[1] * front_res[1]
    share(BWD0, masks[0] * (links[1] * total1))
    front_res[1] = total1
    total0 = front0 + masks[0] * schur(BWD0, 0)

    @pl.when(turn > 0)
    def _():
        passing[1] = links[0] * total0
        hand_on(1, turn - 1).start()

    share(TOT0, total0)
    share(TOT1, total1)
    front_res[0] = total0
    front_store = pltpu.make_async_copy(front_res, front_out, store_sem.at[0])
    front_store.start()

    stores = []
    for p, g in ((1, TOT1), (0, TOT0)):
        picked = product(g, onehot.at[p]).astype(BF16)
        first = lax.dot_general(picked, coupling_v[p, 0], NT, preferred_element_type=F32)
        second = lax.dot_general(picked, coupling_v[p, 1], NT, preferred_element_type=F32)
        lifted = combined(first, second).astype(BF16)
        inner_res[p] = solved_v[p] - combined(dot(lifted, inverse_v[p, 0]), dot(lifted, inverse_v[p, 1]))
        store = pltpu.make_async_copy(inner_res.at[p], inner_out.at[p], store_sem.at[1 + p])
        store.start()
        stores.append(store)

    for p in range(2):
        wait_bytes(parts.at[p, pl.ds(0, peers - 1)], send_sem.at[p])
    for g in (FWD0, FWD1, BWD0, TOT1, TOT0):
        wait_bytes(gathered.at[g, pl.ds(0, peers - 1)], send_sem.at[2 + g])

    @pl.when(turn < depth - 1)
    def _():
        wait_bytes(gathered.at[BWD1, pl.ds(0, peers - 1)], send_sem.at[2 + BWD1])
        hand_on(0, turn + 1).wait_send()

    @pl.when(turn > 0)
    def _():
        hand_on(1, turn - 1).wait_send()

    front_store.wait()
    for store in stores:
        store.wait()


def solution(mesh):
    n_xy = mesh.shape["xy"]
    depth = mesh.shape["gz"]
    side = round((n_xy // 2) ** 0.5)

    def on_device(inner, front, inverse, coupling, schur, rows, link, size):
        panels, two, rhs, loc = inner.shape
        both = two * rhs
        unknowns = schur.shape[2]
        bnd = coupling.shape[-1]
        inverse = inverse.reshape(panels, two, loc, loc)
        coupling = coupling.reshape(panels, two, loc, bnd)
        inner = inner.reshape(panels, both, loc)
        front = front.reshape(panels, both, LANES)
        hbm = pl.BlockSpec(memory_space=pltpu.HBM)
        vmem = pltpu.VMEM
        inner_out, front_out = pl.pallas_call(
            functools.partial(kernel, side, depth),
            out_shape=(
                jax.ShapeDtypeStruct(inner.shape, F32),
                jax.ShapeDtypeStruct(front.shape, F32),
            ),
            in_specs=[hbm] * 7 + [pl.BlockSpec(memory_space=pltpu.SMEM)],
            out_specs=(hbm, hbm),
            scratch_shapes=[
                vmem(inner.shape, F32),
                vmem(front.shape, F32),
                vmem(inverse.shape, BF16),
                vmem(coupling.shape, BF16),
                vmem((panels, unknowns, 2 * LANES), BF16),
                vmem(rows.shape, jnp.int32),
                vmem(link.shape, F32),
                vmem((panels, unknowns, bnd), BF16),
                vmem((panels, n_xy, both, LANES), BF16),
                vmem((panels, n_xy, both, LANES), BF16),
                vmem((6, n_xy, both, LANES), BF16),
                vmem((2, both, LANES), F32),
                vmem((2, both, LANES), F32),
                vmem(inner.shape, F32),
                vmem(inner.shape, F32),
                vmem(front.shape, F32),
                vmem(front.shape, F32),
                pltpu.SemaphoreType.DMA((12,)),
                pltpu.SemaphoreType.DMA((3,)),
                pltpu.SemaphoreType.DMA((8,)),
                pltpu.SemaphoreType.DMA((6, n_xy // 2)),
                pltpu.SemaphoreType.DMA((2,)),
                pltpu.SemaphoreType.DMA((2,)),
                pltpu.SemaphoreType.DMA((2,)),
            ],
            compiler_params=pltpu.CompilerParams(
                collective_id=0, has_side_effects=True, vmem_limit_bytes=60 << 20
            ),
            name="sweep",
        )(inner, front, inverse, coupling, schur, rows, link, size)
        return (
            inner_out.reshape(panels, two, rhs, loc),
            front_out.reshape(panels, two, rhs, LANES),
        )

    placed = (
        P("gz", None, None, "xy"),
        P("gz", None, None, "xy"),
        P("gz", "xy", None, None, None),
        P("gz", "xy", None, None, None),
        P("gz", None, None, "xy"),
        P("gz", "xy"),
        P("gz", "xy"),
        P("gz"),
    )
    return jax.shard_map(
        on_device,
        mesh=mesh,
        in_specs=placed,
        out_specs=(P("gz", None, None, "xy"), P("gz", None, None, "xy")),
        check_vma=False,
    )
```

time: 635 us -> 138 us (0.22)
  blocking collectives: 381 us -> 0 us
  Pallas kernels: 0 us -> 135 us
  waiting for transfers between devices: 101 us -> 0 us
  other arithmetic: 62 us -> 0 us
  local copies, waits for them, and re-layouts: 34 us -> 2.94 us
  matrix products: 24.5 us -> 0 us
  starting transfers between devices: 15 us -> 0 us
  between operations: 14.8 us -> 0.64 us
    all_gather x16 -> x0, blocking collectives: 381 us -> none  [the longest x15 357 us: schur_apply(): lax.all_gather(outgoing, 'xy', axis=2, tiled=True)]
    pallas_call x0 -> x1, Pallas kernels: none -> 135 us  [on_device(): pl.pallas_call(functools.partial(kernel, side, depth), out_shape=(jax.Sha...]
    reduce_scatter x2 -> x0, waiting for transfers between devices: 88.7 us -> none  [on_device(): contrib = lax.psum_scatter(spread, 'xy', scatter_dimension=2, tiled=True)]
    scatter-add x2 -> x0, other arithmetic: 49.6 us -> none  [on_device(): spread = spread.at[:, :, front_rows[panel_index]].add(pushed)]
    dot_general x48 -> x0, matrix products: 24.5 us -> none  [the longest x22 12.5 us: complex_product(): second = jnp.dot(flattened, matrix[1], preferred_element_type=jnp.float32)]
    ppermute x6 -> x0, starting transfers between devices: 15 us -> none  [passed_along(): return lax.ppermute(shard, axis, pairs)]
    ppermute x6 -> x0, waiting for transfers between devices: 12.1 us -> none  [passed_along(): return lax.ppermute(shard, axis, pairs)]
    scatter-add x2 -> x0, local copies, waits for them, and re-layouts: 11.7 us -> none  [on_device(): spread = spread.at[:, :, front_rows[panel_index]].add(pushed)]
  transfers between devices with their start and end apart: 8 -> 0, of which waited for: 8 -> 0; matrix products, arithmetic and copies ran while one was open for 7% -> 0% of each run, Pallas kernels for 0% -> 0%
where the time goes in v1:
time: 138 us
  Pallas kernels  135 us (98%)
  local copies, waits for them, and re-layouts  2.94 us (2%)
    pallas_call x1, Pallas kernels, on_device(): pl.pallas_call(functools.partial(kernel, side, depth), out_shape=(jax.Sha...  135 us
    unnamed x2, local copies, waits for them, and re-layouts  2.94 us

profile of v1, /device:TPU:1, one launch (start us, length us, event | category | flops | bytes accessed | tf_op | source)
XLA Modules:
  0.0 138.2 jit_solution(15816986011292820505)
XLA Ops:
  0.6 134.6 %sweep.1 = (f32[2,32,512]{2,1,0:T(8,128)}, f32[2,32,128]{2,1,0:T(8,128)}) custom-call(f32[2,32,512]{2,1,0:T(8,128)} %bitcast.8, f32[2,32,128]{2,1,0:T(8,128)} %bitcast.10, bf16[2,2,512,512]{3,2,1,0:T(8,128)(2,1)} %bitcast.6, bf16[2,2,512,256]{3,2,1,0:T(8,128)(2,1)} %bitcast.7, bf16[2,2,4096,128]{3,2,1,0:T(8,128)(2,1)} %schur_hbm.1, s32[2,256]{1,0:T(2,128)} %rows_hbm.1, ...), custom_call_target="tpu_custom_call" | custom-call | tf_op jit(solution)/shard_map/sweep/pallas_call | solution.py:313
  135.2 1.6 %copy.12 = f32[2,2,16,512]{3,2,1,0:T(8,128)} copy(f32[2,2,16,512]{3,2,1,0:T(8,128)} %bitcast.9) | data formatting | bytes 262144
  136.8 1.4 copy.13

commit v2 on v1

v2 whole, which is shorter than its diff:
```python
import functools

import jax
import jax.numpy as jnp
from jax import lax
from jax.experimental import pallas as pl
from jax.experimental.pallas import tpu as pltpu
from jax.sharding import PartitionSpec as P

MESH = pl.DeviceIdType.MESH
F32 = jnp.float32
BF16 = jnp.bfloat16
NT = (((1,), (1,)), ((), ()))
LANES = 128

ROWS = 16
HALVES = 2
FWD0, FWD1, BWD1, BWD0, TOT1, TOT0 = range(6)


def dot(a, b):
    return jnp.dot(a, b, preferred_element_type=F32)


def dot_t(a, b):
    return lax.dot_general(a, b, NT, preferred_element_type=F32)


def combined(first, second):
    pieces = []
    for start in range(0, first.shape[0], ROWS):
        mid, end = start + ROWS // 2, start + ROWS
        pieces += [first[start:mid] - second[mid:end], second[start:mid] + first[mid:end]]
    return jnp.concatenate(pieces, axis=0)


def kernel(
    side,
    depth,
    inner_hbm,
    front_hbm,
    inverse_hbm,
    coupling_hbm,
    schur_hbm,
    rows_hbm,
    link_hbm,
    size_ref,
    inner_out,
    front_out,
    inner_v,
    front_v,
    inverse_v,
    coupling_v,
    schur_v,
    rows_v,
    link_v,
    onehot,
    parts,
    landed,
    gathered,
    crossing,
    ahead,
    ahead_in,
    mask_out,
    mask_in,
    base_v,
    first_v,
    last_v,
    solved_v,
    inner_res,
    front_res,
    load_sem,
    store_sem,
    contrib_send,
    contrib_sem,
    gather_send,
    gather_sem,
    cross_send,
    near_send,
    near_sem,
    side_send,
    side_sem,
):
    chips = side * side
    peers = 2 * chips
    me = lax.axis_index("xy")
    turn = lax.axis_index("gz")
    core = lax.rem(me, 2)
    chip = me // 2
    chip_x = chip // side
    chip_y = lax.rem(chip, side)

    def chip_at(dx, dy):
        return lax.rem(chip_x + dx, side) * side + lax.rem(chip_y + dy, side)

    def distance(d):
        return min(d, side - d)

    offsets = sorted(
        ((dx, dy) for dx in range(side) for dy in range(side)),
        key=lambda d: (distance(d[0]) + distance(d[1]), d),
    )
    near_chips = [chip_at(*d) for d in offsets]
    far_first = [
        2 * c + lax.rem(core + q, 2) for c in reversed(near_chips[1:]) for q in range(2)
    ] + [2 * chip + 1 - core]

    loads = []

    def load(src, dst):
        copy = pltpu.make_async_copy(src, dst, load_sem.at[len(loads)])
        copy.start()
        loads.append(copy)
        return copy

    rows_load = load(rows_hbm, rows_v)
    inner_load = load(inner_hbm, inner_v)
    local_loads = []
    for p in range(2):
        local_loads.append((load(inverse_hbm.at[p], inverse_v.at[p]), load(coupling_hbm.at[p], coupling_v.at[p])))
    front_load = load(front_hbm, front_v)
    link_load = load(link_hbm, link_v)
    schur_loads = [
        [load(schur_hbm.at[p, i], schur_v.at[p, :, pl.ds(i * LANES, LANES)]) for i in range(2)]
        for p in range(2)
    ]

    barrier = pltpu.get_barrier_semaphore()

    def greet(where):
        pl.semaphore_signal(barrier, inc=1, device_id=where, device_id_type=MESH)

    for peer in far_first:
        greet({"xy": peer})

    @pl.when(turn > 0)
    def _():
        for peer in far_first + [me]:
            greet({"xy": peer, "gz": turn - 1})

    @pl.when(turn < depth - 1)
    def _():
        for peer in far_first + [me]:
            greet({"xy": peer, "gz": turn + 1})

    def wait_bytes(ref, sem):
        pltpu.make_async_copy(ref, ref, sem).wait()

    def halves_of(ref, p):
        return jnp.concatenate([ref[p, i, h] for h in range(HALVES) for i in range(2)], axis=0)

    def local_part(p):
        iota = lax.broadcasted_iota(jnp.int32, (2 * LANES, 2 * LANES), 0)
        wanted = rows_v[p : p + 1, :]
        for c in range(chips):
            onehot[p, pl.ds(c * 2 * LANES, 2 * LANES), :] = (
                iota + c * 2 * LANES == wanted
            ).astype(F32).astype(BF16)
        for copy in local_loads[p]:
            copy.wait()
        field = halves_of(inner_v, p).astype(BF16)
        solved = combined(dot(field, inverse_v[p, 0]), dot(field, inverse_v[p, 1]))
        solved_v[p] = solved
        rounded = solved.astype(BF16)
        pushed = combined(dot(rounded, coupling_v[p, 0]), dot(rounded, coupling_v[p, 1])).astype(BF16)
        for c in range(chips):
            spread = dot_t(pushed, onehot[p, pl.ds(c * 2 * LANES, 2 * LANES), :]).astype(BF16)
            for h in range(HALVES):
                for q in range(2):
                    parts[p, h, 2 * c + q] = spread[h * ROWS : (h + 1) * ROWS, q * LANES : (q + 1) * LANES]
        for h in range(HALVES):
            landed[p, h, me] = parts[p, h, me]

    def send_parts(p):
        for h in range(HALVES):
            for peer in far_first:
                pltpu.make_async_remote_copy(
                    src_ref=parts.at[p, h, peer],
                    dst_ref=landed.at[p, h, me],
                    send_sem=contrib_send.at[p, h],
                    recv_sem=contrib_sem.at[p, h],
                    device_id={"xy": peer},
                    device_id_type=MESH,
                ).start()

    rows_load.wait()
    inner_load.wait()
    local_part(0)
    pl.semaphore_wait(
        barrier, peers - 1 + peers * (jnp.minimum(turn, 1) + jnp.minimum(depth - 1 - turn, 1))
    )
    send_parts(0)
    local_part(1)
    send_parts(1)
    front_load.wait()
    link_load.wait()

    own = me * LANES + lax.broadcasted_iota(jnp.int32, (1, LANES), 1)
    masks = [jnp.where(own < size_ref[p], 1.0, 0.0).astype(F32) for p in range(2)]
    links = [link_v[p : p + 1, :] for p in range(2)]

    def to_next():
        return pltpu.make_async_remote_copy(
            src_ref=mask_out,
            dst_ref=mask_in,
            send_sem=side_send.at[0],
            recv_sem=side_sem.at[0],
            device_id={"gz": turn + 1},
            device_id_type=MESH,
        )

    def to_previous():
        return pltpu.make_async_remote_copy(
            src_ref=ahead,
            dst_ref=ahead_in,
            send_sem=side_send.at[1],
            recv_sem=side_sem.at[1],
            device_id={"gz": turn - 1},
            device_id_type=MESH,
        )

    @pl.when(turn < depth - 1)
    def _():
        mask_out[...] = jnp.broadcast_to(masks[1], mask_out.shape)
        to_next().start()

    def share(g, h, block):
        gathered[g, h, me] = block.astype(BF16)
        for peer in far_first:
            pltpu.make_async_remote_copy(
                src_ref=gathered.at[g, h, me],
                dst_ref=gathered.at[g, h, me],
                send_sem=gather_send.at[g, h],
                recv_sem=gather_sem.at[g, h, chip],
                device_id={"xy": peer},
                device_id_type=MESH,
            ).start()

    near = sum(sum(map(distance, d)) < 2 for d in offsets)
    cross_order = far_first[: 2 * (chips - near)] + [2 * c + core for c in reversed(near_chips[:near])]

    def cross(i, g, h, block, to):
        crossing[i, h] = block.astype(BF16)
        for peer in cross_order:
            pltpu.make_async_remote_copy(
                src_ref=crossing.at[i, h],
                dst_ref=gathered.at[g, h, me],
                send_sem=cross_send.at[i, h],
                recv_sem=gather_sem.at[g, h, chip],
                device_id={"xy": peer, "gz": to},
                device_id_type=MESH,
            ).start()

    def base_of(p, h):
        wait_bytes(landed.at[p, h, pl.ds(0, peers - 1)], contrib_sem.at[p, h])
        total = landed[p, h, 0].astype(F32)
        for i in range(1, peers):
            total = total + landed[p, h, i].astype(F32)
        return jnp.concatenate([front_v[p, i, h] for i in range(2)], axis=0) - total

    for h in range(HALVES):
        base = base_of(0, h)
        masked = masks[0] * base

        @pl.when(turn == 0)
        def _():
            share(FWD0, h, masks[0] * (base + links[0] * jnp.zeros_like(base)))

        @pl.when(turn > 0)
        def _():
            ahead[pl.ds(h * ROWS, ROWS), :] = masked

    @pl.when(turn > 0)
    def _():
        ahead[pl.ds(HALVES * ROWS, 8), :] = jnp.broadcast_to(masks[0] * links[0], (8, LANES))
        to_previous().start()

    for h in range(HALVES):
        base_v[h] = base_of(1, h)
    for p in range(2):
        for copy in schur_loads[p]:
            copy.wait()

    def product(g, h, matrix, arrival):
        total = None
        for i, c in enumerate(near_chips):
            if arrival is not None:
                arrival(g, h, i, c)
            block = jnp.concatenate([gathered[g, h, 2 * c], gathered[g, h, 2 * c + 1]], axis=1)
            rows = pl.ds(pl.multiple_of(c * 2 * LANES, 2 * LANES), 2 * LANES)
            term = dot(block, matrix[rows, :])
            total = term if total is None else total + term
        return total

    def shared(g, h, i, c):
        wait_bytes(gathered.at[g, h, pl.ds(0, 1 if i == 0 else 2)], gather_sem.at[g, h, c])

    def handed(i, g, h, j):
        slot = 2 * near_chips[j] + core
        return pltpu.make_async_remote_copy(
            src_ref=gathered.at[g, h, slot],
            dst_ref=gathered.at[g, h, slot],
            send_sem=near_send.at[i, h],
            recv_sem=near_sem.at[i, h, j],
            device_id={"xy": 2 * chip + 1 - core},
            device_id_type=MESH,
        )

    def hand_over(i, g, h):
        for j in range(near):
            wait_bytes(gathered.at[g, h, 0], gather_sem.at[g, h, near_chips[j]])
            handed(i, g, h, j).start()

    def crossed(i):
        def wait(g, h, j, c):
            if j < near:
                wait_bytes(gathered.at[g, h, 0], near_sem.at[i, h, j])
            else:
                wait_bytes(gathered.at[g, h, pl.ds(0, 2)], gather_sem.at[g, h, c])

        return wait

    def schur(g, h, p, arrival):
        out = product(g, h, schur_v.at[p], arrival)
        return combined(out[:, :LANES], out[:, LANES:])

    @pl.when(turn == depth - 1)
    def _():
        for h in range(HALVES):
            for i in range(peers):
                gathered[BWD1, h, i] = jnp.zeros((ROWS, LANES), BF16)
            last_v[h] = masks[1] * schur(BWD1, h, 1, None)

    for h in range(HALVES):

        @pl.when(turn == 0)
        def _():
            first_v[h] = masks[0] * schur(FWD0, h, 0, shared)

        @pl.when(turn > 0)
        def _():
            hand_over(0, FWD0, h)
            first_v[h] = masks[0] * schur(FWD0, h, 0, crossed(0))

        front = first_v[h]
        share(FWD1, h, masks[1] * (base_v[h] + links[1] * front))

    @pl.when(turn < depth - 1)
    def _():
        pltpu.make_async_copy(ahead_in, ahead_in, side_sem.at[1]).wait()

    for h in range(HALVES):
        front = masks[1] * schur(FWD1, h, 1, shared)

        @pl.when(turn < depth - 1)
        def _():
            cross(
                0,
                FWD0,
                h,
                ahead_in[pl.ds(h * ROWS, ROWS), :] + ahead_in[pl.ds(HALVES * ROWS, 1), :] * front,
                turn + 1,
            )
            last_v[h] = front

        @pl.when(turn == depth - 1)
        def _():
            total = front + last_v[h]
            share(BWD0, h, masks[0] * (links[1] * total))
            last_v[h] = total

    @pl.when(turn < depth - 1)
    def _():
        for h in range(HALVES):
            hand_over(1, BWD1, h)
            total = last_v[h] + masks[1] * schur(BWD1, h, 1, crossed(1))
            share(BWD0, h, masks[0] * (links[1] * total))
            last_v[h] = total

    @pl.when(turn == 0)
    def _():
        for h in range(HALVES):
            share(TOT1, h, last_v[h])

    @pl.when(turn > 0)
    def _():
        pltpu.make_async_copy(mask_in, mask_in, side_sem.at[0]).wait()

    for h in range(HALVES):
        total = first_v[h] + masks[0] * schur(BWD0, h, 0, shared)
        first_v[h] = total

        @pl.when(turn > 0)
        def _():
            cross(1, BWD1, h, mask_in[0:1, :] * (links[0] * total), turn - 1)

        @pl.when(turn == 0)
        def _():
            share(TOT0, h, total)

    @pl.when(turn > 0)
    def _():
        for h in range(HALVES):
            share(TOT0, h, first_v[h])
        for h in range(HALVES):
            share(TOT1, h, last_v[h])

    for h in range(HALVES):
        for i in range(2):
            rows = pl.ds(i * (ROWS // 2), ROWS // 2)
            front_res[0, i, h] = first_v[h, rows, :]
            front_res[1, i, h] = last_v[h, rows, :]
    stores = [pltpu.make_async_copy(front_res, front_out, store_sem.at[0])]
    stores[0].start()

    for p, g in ((1, TOT1), (0, TOT0)):
        for h in range(HALVES):
            picked = product(g, h, onehot.at[p], shared).astype(BF16)
            lifted = combined(dot_t(picked, coupling_v[p, 0]), dot_t(picked, coupling_v[p, 1])).astype(BF16)
            inner = solved_v[p, pl.ds(h * ROWS, ROWS), :] - combined(
                dot(lifted, inverse_v[p, 0]), dot(lifted, inverse_v[p, 1])
            )
            for i in range(2):
                inner_res[p, i, h] = inner[i * (ROWS // 2) : (i + 1) * (ROWS // 2)]
        store = pltpu.make_async_copy(inner_res.at[p], inner_out.at[p], store_sem.at[1 + p])
        store.start()
        stores.append(store)

    for h in range(HALVES):
        for p in range(2):
            wait_bytes(parts.at[p, h, pl.ds(0, peers - 1)], contrib_send.at[p, h])
        for g in (FWD1, BWD0, TOT1, TOT0):
            wait_bytes(gathered.at[g, h, pl.ds(0, peers - 1)], gather_send.at[g, h])

    @pl.when(turn == 0)
    def _():
        for h in range(HALVES):
            wait_bytes(gathered.at[FWD0, h, pl.ds(0, peers - 1)], gather_send.at[FWD0, h])

    @pl.when(turn < depth - 1)
    def _():
        for h in range(HALVES):
            wait_bytes(gathered.at[FWD0, h, pl.ds(0, len(cross_order))], cross_send.at[0, h])
            wait_bytes(gathered.at[BWD1, h, pl.ds(0, near)], near_send.at[1, h])
        to_next().wait_send()

    @pl.when(turn > 0)
    def _():
        for h in range(HALVES):
            wait_bytes(gathered.at[BWD1, h, pl.ds(0, len(cross_order))], cross_send.at[1, h])
            wait_bytes(gathered.at[FWD0, h, pl.ds(0, near)], near_send.at[0, h])
        to_previous().wait_send()

    for store in stores:
        store.wait()


def solution(mesh):
    n_xy = mesh.shape["xy"]
    depth = mesh.shape["gz"]
    side = round((n_xy // 2) ** 0.5)

    def on_device(inner, front, inverse, coupling, schur, rows, link, size):
        panels, two, rhs, loc = inner.shape
        unknowns = schur.shape[2]
        bnd = coupling.shape[-1]
        both = two * rhs
        inverse = inverse.reshape(panels, two, loc, loc)
        coupling = coupling.reshape(panels, two, loc, bnd)
        inner = inner.reshape(panels, two, HALVES, rhs // HALVES, loc)
        front = front.reshape(panels, two, HALVES, rhs // HALVES, LANES)
        hbm = pl.BlockSpec(memory_space=pltpu.HBM)
        vmem = pltpu.VMEM
        dma = pltpu.SemaphoreType.DMA
        inner_out, front_out = pl.pallas_call(
            functools.partial(kernel, side, depth),
            out_shape=(
                jax.ShapeDtypeStruct(inner.shape, F32),
                jax.ShapeDtypeStruct(front.shape, F32),
            ),
            in_specs=[hbm] * 7 + [pl.BlockSpec(memory_space=pltpu.SMEM)],
            out_specs=(hbm, hbm),
            scratch_shapes=[
                vmem(inner.shape, F32),
                vmem(front.shape, F32),
                vmem(inverse.shape, BF16),
                vmem(coupling.shape, BF16),
                vmem((panels, unknowns, 2 * LANES), BF16),
                vmem(rows.shape, jnp.int32),
                vmem(link.shape, F32),
                vmem((panels, unknowns, bnd), BF16),
                vmem((panels, HALVES, n_xy, ROWS, LANES), BF16),
                vmem((panels, HALVES, n_xy, ROWS, LANES), BF16),
                vmem((6, HALVES, n_xy, ROWS, LANES), BF16),
                vmem((2, HALVES, ROWS, LANES), BF16),
                vmem((HALVES * ROWS + 8, LANES), F32),
                vmem((HALVES * ROWS + 8, LANES), F32),
                vmem((8, LANES), F32),
                vmem((8, LANES), F32),
                vmem((HALVES, ROWS, LANES), F32),
                vmem((HALVES, ROWS, LANES), F32),
                vmem((HALVES, ROWS, LANES), F32),
                vmem((panels, both, loc), F32),
                vmem(inner.shape, F32),
                vmem(front.shape, F32),
                dma((12,)),
                dma((3,)),
                dma((2, HALVES)),
                dma((2, HALVES)),
                dma((6, HALVES)),
                dma((6, HALVES, n_xy // 2)),
                dma((2, HALVES)),
                dma((2, HALVES)),
                dma((2, HALVES, 5)),
                dma((2,)),
                dma((2,)),
            ],
            compiler_params=pltpu.CompilerParams(
                collective_id=0, has_side_effects=True, vmem_limit_bytes=60 << 20
            ),
            name="sweep",
        )(inner, front, inverse, coupling, schur, rows, link, size)
        return (
            inner_out.reshape(panels, two, rhs, loc),
            front_out.reshape(panels, two, rhs, LANES),
        )

    placed = (
        P("gz", None, None, "xy"),
        P("gz", None, None, "xy"),
        P("gz", "xy", None, None, None),
        P("gz", "xy", None, None, None),
        P("gz", None, None, "xy"),
        P("gz", "xy"),
        P("gz", "xy"),
        P("gz"),
    )
    return jax.shard_map(
        on_device,
        mesh=mesh,
        in_specs=placed,
        out_specs=(P("gz", None, None, "xy"), P("gz", None, None, "xy")),
        check_vma=False,
    )
```

time: 138 us -> 117 us (0.85)
  Pallas kernels: 135 us -> 113 us
    pallas_call x1, Pallas kernels: 135 us -> 113 us  [on_device(): pl.pallas_call(functools.partial(kernel, side, depth), out_shape=(jax.Sha...]
where the time goes in v2:
time: 117 us
  Pallas kernels  113 us (97%)
  local copies, waits for them, and re-layouts  2.94 us (3%)
    pallas_call x1, Pallas kernels, on_device(): pl.pallas_call(functools.partial(kernel, side, depth), out_shape=(jax.Sha...  113 us
    unnamed x2, local copies, waits for them, and re-layouts  2.94 us

profile of v2, /device:TPU:1, one launch (start us, length us, event | category | flops | bytes accessed | tf_op | source)
XLA Modules:
  0.0 116.9 jit_solution(7064146208884040826)
XLA Ops:
  0.6 113.3 %sweep.1 = (f32[2,2,2,8,512]{4,3,2,1,0:T(8,128)}, f32[2,2,2,8,128]{4,3,2,1,0:T(8,128)}) custom-call(f32[2,2,2,8,512]{4,3,2,1,0:T(8,128)} %bitcast.8, f32[2,2,2,8,128]{4,3,2,1,0:T(8,128)} %bitcast.10, bf16[2,2,512,512]{3,2,1,0:T(8,128)(2,1)} %bitcast.6, bf16[2,2,512,256]{3,2,1,0:T(8,128)(2,1)} %bitcast.7, bf16[2,2,4096,128]{3,2,1,0:T(8,128)(2,1)} %schur_hbm.1, ...), custom_call_target="tpu_custom_call" | custom-call | tf_op jit(solution)/shard_map/sweep/pallas_call | solution.py:475
  114.0 1.6 %copy.12 = f32[2,2,16,512]{3,2,1,0:T(8,128)} copy(f32[2,2,16,512]{3,2,1,0:T(8,128)} %bitcast.9) | data formatting | bytes 262144
  115.5 1.4 %copy.13 = f32[2,2,16,128]{3,2,1,0:T(8,128)} copy(f32[2,2,16,128]{3,2,1,0:T(8,128)} %bitcast.11) | data formatting | bytes 65536

commit v3 on v2

--- a/solution.py
+++ b/solution.py
@@ -44,7 +44,7 @@
     schur_hbm,
     rows_hbm,
     link_hbm,
-    size_ref,
+    size_hbm,
     inner_out,
     front_out,
     inner_v,
@@ -54,6 +54,7 @@
     schur_v,
     rows_v,
     link_v,
+    size_ref,
     onehot,
     parts,
     landed,
@@ -120,6 +121,7 @@
         local_loads.append((load(inverse_hbm.at[p], inverse_v.at[p]), load(coupling_hbm.at[p], coupling_v.at[p])))
     front_load = load(front_hbm, front_v)
     link_load = load(link_hbm, link_v)
+    size_load = load(size_hbm, size_ref)
     schur_loads = [
         [load(schur_hbm.at[p, i], schur_v.at[p, :, pl.ds(i * LANES, LANES)]) for i in range(2)]
         for p in range(2)
@@ -135,13 +137,11 @@
 
     @pl.when(turn > 0)
     def _():
-        for peer in far_first + [me]:
-            greet({"xy": peer, "gz": turn - 1})
+        greet({"gz": turn - 1})
 
     @pl.when(turn < depth - 1)
     def _():
-        for peer in far_first + [me]:
-            greet({"xy": peer, "gz": turn + 1})
+        greet({"gz": turn + 1})
 
     def wait_bytes(ref, sem):
         pltpu.make_async_copy(ref, ref, sem).wait()
@@ -187,13 +187,14 @@
     inner_load.wait()
     local_part(0)
     pl.semaphore_wait(
-        barrier, peers - 1 + peers * (jnp.minimum(turn, 1) + jnp.minimum(depth - 1 - turn, 1))
+        barrier, peers - 1 + jnp.minimum(turn, 1) + jnp.minimum(depth - 1 - turn, 1)
     )
     send_parts(0)
     local_part(1)
     send_parts(1)
     front_load.wait()
     link_load.wait()
+    size_load.wait()
 
     own = me * LANES + lax.broadcasted_iota(jnp.int32, (1, LANES), 1)
     masks = [jnp.where(own < size_ref[p], 1.0, 0.0).astype(F32) for p in range(2)]
@@ -410,6 +411,7 @@
             rows = pl.ds(i * (ROWS // 2), ROWS // 2)
             front_res[0, i, h] = first_v[h, rows, :]
             front_res[1, i, h] = last_v[h, rows, :]
+
     stores = [pltpu.make_async_copy(front_res, front_out, store_sem.at[0])]
     stores[0].start()
 
@@ -422,6 +424,7 @@
             )
             for i in range(2):
                 inner_res[p, i, h] = inner[i * (ROWS // 2) : (i + 1) * (ROWS // 2)]
+
         store = pltpu.make_async_copy(inner_res.at[p], inner_out.at[p], store_sem.at[1 + p])
         store.start()
         stores.append(store)
@@ -451,6 +454,19 @@
             wait_bytes(gathered.at[FWD0, h, pl.ds(0, near)], near_send.at[0, h])
         to_previous().wait_send()
 
+    for store in stores:
+        store.wait()
+
+
+def put(inner_in, front_in, inner_out, front_out, inner_v, front_v, sem):
+    pairs = ((inner_in, inner_v, inner_out), (front_in, front_v, front_out))
+    loads = [pltpu.make_async_copy(src, held, sem.at[0, i]) for i, (src, held, _) in enumerate(pairs)]
+    stores = [pltpu.make_async_copy(held, dst, sem.at[1, i]) for i, (_, held, dst) in enumerate(pairs)]
+    for copy in loads:
+        copy.start()
+    for copy, store in zip(loads, stores):
+        copy.wait()
+        store.start()
     for store in stores:
         store.wait()
 
@@ -478,7 +494,7 @@
                 jax.ShapeDtypeStruct(inner.shape, F32),
                 jax.ShapeDtypeStruct(front.shape, F32),
             ),
-            in_specs=[hbm] * 7 + [pl.BlockSpec(memory_space=pltpu.SMEM)],
+            in_specs=[hbm] * 8,
             out_specs=(hbm, hbm),
             scratch_shapes=[
                 vmem(inner.shape, F32),
@@ -488,6 +504,7 @@
                 vmem((panels, unknowns, 2 * LANES), BF16),
                 vmem(rows.shape, jnp.int32),
                 vmem(link.shape, F32),
+                pltpu.SMEM(size.shape, jnp.int32),
                 vmem((panels, unknowns, bnd), BF16),
                 vmem((panels, HALVES, n_xy, ROWS, LANES), BF16),
                 vmem((panels, HALVES, n_xy, ROWS, LANES), BF16),
@@ -503,7 +520,7 @@
                 vmem((panels, both, loc), F32),
                 vmem(inner.shape, F32),
                 vmem(front.shape, F32),
-                dma((12,)),
+                dma((13,)),
                 dma((3,)),
                 dma((2, HALVES)),
                 dma((2, HALVES)),
@@ -520,6 +537,18 @@
             ),
             name="sweep",
         )(inner, front, inverse, coupling, schur, rows, link, size)
+        inner_out, front_out = pl.pallas_call(
+            put,
+            out_shape=(
+                jax.ShapeDtypeStruct(inner.shape, F32),
+                jax.ShapeDtypeStruct(front.shape, F32),
+            ),
+            in_specs=[hbm, hbm],
+            out_specs=(hbm, hbm),
+            scratch_shapes=[vmem(inner.shape, F32), vmem(front.shape, F32), dma((2, 2))],
+            compiler_params=pltpu.CompilerParams(vmem_limit_bytes=60 << 20),
+            name="put",
+        )(inner_out, front_out)
         return (
             inner_out.reshape(panels, two, rhs, loc),
             front_out.reshape(panels, two, rhs, LANES),

time: 117 us -> 113 us (0.966)
  local copies, waits for them, and re-layouts: 2.94 us -> 0 us
    pallas_call x1, Pallas kernels: 113 us -> 110 us  [on_device(): pl.pallas_call(functools.partial(kernel, side, depth), out_shape=(jax.Sha...]
    unnamed x2 -> x0, local copies, waits for them, and re-layouts: 2.94 us -> none
    pallas_call x0 -> x1, Pallas kernels: none -> 1.6 us  [on_device(): pl.pallas_call(put, out_shape=(jax.ShapeDtypeStruct(inner.shape, F32), ja...]
where the time goes in v3:
time: 113 us; the launch traced here: 112 us
  Pallas kernels  112 us (99%)
    pallas_call x1, Pallas kernels, on_device(): pl.pallas_call(functools.partial(kernel, side, depth), out_shape=(jax.Sha...  110 us

profile of v3, /device:TPU:1, one launch (start us, length us, event | category | flops | bytes accessed | tf_op | source)
XLA Modules:
  0.0 112.5 jit_solution(9075591742889740148)
XLA Ops:
  0.6 110.1 %sweep.1 = (f32[2,2,2,8,512]{4,3,2,1,0:T(8,128)}, f32[2,2,2,8,128]{4,3,2,1,0:T(8,128)}) custom-call(f32[2,2,2,8,512]{4,3,2,1,0:T(8,128)} %bitcast.8, f32[2,2,2,8,128]{4,3,2,1,0:T(8,128)} %bitcast.9, bf16[2,2,512,512]{3,2,1,0:T(8,128)(2,1)} %bitcast.6, bf16[2,2,512,256]{3,2,1,0:T(8,128)(2,1)} %bitcast.7, bf16[2,2,4096,128]{3,2,1,0:T(8,128)(2,1)} %schur_hbm.1, ...), custom_call_target="tpu_custom_call" | custom-call | tf_op jit(solution)/shard_map/sweep/pallas_call | solution.py:491
  110.7 1.6 %put.1 = (f32[2,2,2,8,512]{4,3,2,1,0:T(8,128)}, f32[2,2,2,8,128]{4,3,2,1,0:T(8,128)}) custom-call(f32[2,2,2,8,512]{4,3,2,1,0:T(8,128)} %get-tuple-element.6.inner_in, f32[2,2,2,8,128]{4,3,2,1,0:T(8,128)} %get-tuple-element.7.front_in), custom_call_target="tpu_custom_call" | custom-call | tf_op jit(solution)/shard_map/put/pallas_call | solution.py:540

commit v4 on v3

--- a/solution.py
+++ b/solution.py
@@ -282,14 +282,19 @@
         for copy in schur_loads[p]:
             copy.wait()
 
-    def product(g, h, matrix, arrival):
+    middle = sum(sum(map(distance, d)) < 3 for d in offsets)
+    late = list(range(near, middle)) + list(range(near)) + list(range(middle, chips))
+
+    def product(g, h, matrix, arrival, order=None):
         total = None
-        for i, c in enumerate(near_chips):
+        for i in order or range(chips):
+            c = near_chips[i]
+            rows = pl.ds(pl.multiple_of(c * 2 * LANES, 2 * LANES), 2 * LANES)
+            held = matrix[rows, :]
             if arrival is not None:
                 arrival(g, h, i, c)
             block = jnp.concatenate([gathered[g, h, 2 * c], gathered[g, h, 2 * c + 1]], axis=1)
-            rows = pl.ds(pl.multiple_of(c * 2 * LANES, 2 * LANES), 2 * LANES)
-            term = dot(block, matrix[rows, :])
+            term = dot(block, held)
             total = term if total is None else total + term
         return total
 
@@ -321,8 +326,8 @@
 
         return wait
 
-    def schur(g, h, p, arrival):
-        out = product(g, h, schur_v.at[p], arrival)
+    def schur(g, h, p, arrival, order=None):
+        out = product(g, h, schur_v.at[p], arrival, order)
         return combined(out[:, :LANES], out[:, LANES:])
 
     @pl.when(turn == depth - 1)
@@ -341,7 +346,7 @@
         @pl.when(turn > 0)
         def _():
             hand_over(0, FWD0, h)
-            first_v[h] = masks[0] * schur(FWD0, h, 0, crossed(0))
+            first_v[h] = masks[0] * schur(FWD0, h, 0, crossed(0), late)
 
         front = first_v[h]
         share(FWD1, h, masks[1] * (base_v[h] + links[1] * front))
@@ -374,7 +379,7 @@
     def _():
         for h in range(HALVES):
             hand_over(1, BWD1, h)
-            total = last_v[h] + masks[1] * schur(BWD1, h, 1, crossed(1))
+            total = last_v[h] + masks[1] * schur(BWD1, h, 1, crossed(1), late)
             share(BWD0, h, masks[0] * (links[1] * total))
             last_v[h] = total
 

time: 113 us -> 112 us (level)
  no operation moved by 1% of the time
where the time goes in v4:
time: 112 us
  Pallas kernels  111 us (99%)
    pallas_call x1, Pallas kernels, on_device(): pl.pallas_call(functools.partial(kernel, side, depth), out_shape=(jax.Sha...  110 us

profile of v4, /device:TPU:1, one launch (start us, length us, event | category | flops | bytes accessed | tf_op | source)
XLA Modules:
  0.0 112.0 jit_solution(5636132758674786940)
XLA Ops:
  0.6 109.6 %sweep.1 = (f32[2,2,2,8,512]{4,3,2,1,0:T(8,128)}, f32[2,2,2,8,128]{4,3,2,1,0:T(8,128)}) custom-call(f32[2,2,2,8,512]{4,3,2,1,0:T(8,128)} %bitcast.8, f32[2,2,2,8,128]{4,3,2,1,0:T(8,128)} %bitcast.9, bf16[2,2,512,512]{3,2,1,0:T(8,128)(2,1)} %bitcast.6, bf16[2,2,512,256]{3,2,1,0:T(8,128)(2,1)} %bitcast.7, bf16[2,2,4096,128]{3,2,1,0:T(8,128)(2,1)} %schur_hbm.1, ...), custom_call_target="tpu_custom_call" | custom-call | tf_op jit(solution)/shard_map/sweep/pallas_call | solution.py:496
  110.2 1.6 %put.1 = (f32[2,2,2,8,512]{4,3,2,1,0:T(8,128)}, f32[2,2,2,8,128]{4,3,2,1,0:T(8,128)}) custom-call(f32[2,2,2,8,512]{4,3,2,1,0:T(8,128)} %get-tuple-element.6.inner_in, f32[2,2,2,8,128]{4,3,2,1,0:T(8,128)} %get-tuple-element.7.front_in), custom_call_target="tpu_custom_call" | custom-call | tf_op jit(solution)/shard_map/put/pallas_call | solution.py:545

commit v5 on v4

--- a/solution.py
+++ b/solution.py
@@ -383,10 +383,9 @@
             share(BWD0, h, masks[0] * (links[1] * total))
             last_v[h] = total
 
-    @pl.when(turn == 0)
-    def _():
-        for h in range(HALVES):
-            share(TOT1, h, last_v[h])
+            @pl.when(turn == 0)
+            def _():
+                share(TOT1, h, total)
 
     @pl.when(turn > 0)
     def _():

time: 112 us -> 112 us (level)
  no operation moved by 1% of the time
where the time goes in v5:
time: 112 us
  Pallas kernels  111 us (99%)
    pallas_call x1, Pallas kernels, on_device(): pl.pallas_call(functools.partial(kernel, side, depth), out_shape=(jax.Sha...  109 us

profile of v5, /device:TPU:1, one launch (start us, length us, event | category | flops | bytes accessed | tf_op | source)
XLA Modules:
  0.0 111.6 jit_solution(16370987148767632572)
XLA Ops:
  0.6 109.2 %sweep.1 = (f32[2,2,2,8,512]{4,3,2,1,0:T(8,128)}, f32[2,2,2,8,128]{4,3,2,1,0:T(8,128)}) custom-call(f32[2,2,2,8,512]{4,3,2,1,0:T(8,128)} %bitcast.8, f32[2,2,2,8,128]{4,3,2,1,0:T(8,128)} %bitcast.9, bf16[2,2,512,512]{3,2,1,0:T(8,128)(2,1)} %bitcast.6, bf16[2,2,512,256]{3,2,1,0:T(8,128)(2,1)} %bitcast.7, bf16[2,2,4096,128]{3,2,1,0:T(8,128)(2,1)} %schur_hbm.1, ...), custom_call_target="tpu_custom_call" | custom-call | tf_op jit(solution)/shard_map/sweep/pallas_call | solution.py:495
  109.9 1.6 %put.1 = (f32[2,2,2,8,512]{4,3,2,1,0:T(8,128)}, f32[2,2,2,8,128]{4,3,2,1,0:T(8,128)}) custom-call(f32[2,2,2,8,512]{4,3,2,1,0:T(8,128)} %get-tuple-element.6.inner_in, f32[2,2,2,8,128]{4,3,2,1,0:T(8,128)} %get-tuple-element.7.front_in), custom_call_target="tpu_custom_call" | custom-call | tf_op jit(solution)/shard_map/put/pallas_call | solution.py:544
